TPU v7x, 128 devices: a whole 4x4x4 slice. The times are simulated.
128 devices in a mesh: ent: 32 (over x_hi, z, y), sec: 4 (over x_lo, core).
Axes of the slice: x: 4 (x_hi: 2, x_lo: 2; x = x_hi * 2 + x_lo), y: 4, z: 4, core: 2. Of those that a mesh axis runs over, the one named last changes fastest.
Arguments:
- features: bfloat16 [4096, 256], P('ent'), may hold values from -6 to 6
- theta: bfloat16 [256, 256], replicated, may hold values from -3 to 3
- section_weight: float32 [65536], P(('ent', 'sec')), may hold values from 0.5 to 2
- pair_rows: int32 [128, 32, 512], P(('ent', 'sec')), may hold values from 0 to 511
- pair_cols: int32 [128, 32, 512], P(('ent', 'sec')), may hold values from 0 to 127
- pair_counts: int32 [128, 32], P(('ent', 'sec')), may hold values from 0 to 512, as said below
- cotangent: bfloat16 [4096, 256], P('ent'), may hold values from -24 to 24
Outputs:
- activated: bfloat16 [4096, 256], P('ent')
- grad_features: bfloat16 [4096, 256], P('ent')
- grad_theta: float32 [256, 256], replicated
- grad_weight: float32 [65536], P(('ent', 'sec'))
Inputs may be any that keep to these rules, and one draw needn't show every extreme that they name: Only the first pair_counts[k, j] slots of shard k and block j are used; some shard uses all 512 slots of some block.
All inputs are finite; a program needn't handle non-finite values.
Results may differ from a plain program's by a relative error of at most 0.0059.
Values may be sent and summed in bfloat16 or wider, within the bound.
A program may use at most 64 MiB of HBM per device.

v0:
```python
import jax
import jax.numpy as jnp
from jax import lax
from jax.sharding import PartitionSpec as P


def hot_table(indices, live_slots, offset, table_width):
    hits = (indices - offset)[:, None] == jnp.arange(table_width, dtype=jnp.int32)[None, :]
    return (hits & live_slots[:, None]).astype(jnp.bfloat16)


def body(features, theta, section_weight, pair_rows, pair_cols, pair_counts, cotangent):
    ent_dev = features.shape[0]
    feature_width = features.shape[1]
    sec_dev = section_weight.shape[0]
    blocks_count = pair_rows.shape[1]
    slot_count = pair_rows.shape[2]
    own_block = lax.axis_index("ent")
    row_lists = pair_rows[0]
    col_lists = pair_cols[0]
    usable = jnp.arange(slot_count, dtype=jnp.int32)[None, :] < pair_counts[0][:, None]
    usable_float = usable.astype(jnp.float32)
    entity_index = jnp.arange(blocks_count, dtype=jnp.int32)[:, None] * ent_dev + col_lists
    local_degree = jax.ops.segment_sum(
        usable_float.reshape(-1), entity_index.reshape(-1), num_segments=blocks_count * ent_dev
    )
    entity_degree = lax.psum(local_degree, ("ent", "sec"))
    own_degree = lax.dynamic_slice_in_dim(entity_degree, own_block * ent_dev, ent_dev)
    entity_scale = lax.rsqrt(1.0 + own_degree)[:, None]
    sec_count = jax.ops.segment_sum(
        usable_float.reshape(-1), row_lists.reshape(-1), num_segments=sec_dev
    )
    section_scale = (section_weight / (1.0 + sec_count))[:, None]

    def entity_fold(running, incoming, start_row):
        row_count = incoming.shape[0]
        span_width = min(row_count, ent_dev)
        block_span = max(row_count // ent_dev, 1)
        offset = start_row

        def add_block(turn_index, accum):
            row_slots = lax.dynamic_index_in_dim(row_lists, turn_index, 0, keepdims=False)
            col_slots = lax.dynamic_index_in_dim(col_lists, turn_index, 0, keepdims=False)
            live_slots = lax.dynamic_index_in_dim(usable, turn_index, 0, keepdims=False)
            values = lax.dynamic_slice_in_dim(incoming, turn_index * span_width, span_width, 0)
            col_hot = hot_table(col_slots, live_slots, offset, span_width)
            row_hot = hot_table(row_slots, live_slots, 0, sec_dev)
            picked = jnp.dot(col_hot, values, preferred_element_type=jnp.float32).astype(
                jnp.bfloat16
            )
            return accum + jnp.einsum(
                "ps,pf->sf", row_hot, picked, preferred_element_type=jnp.float32
            )

        return lax.fori_loop(0, block_span, add_block, running)

    def entity_terms(messages, start_row):
        span_width = min(lax.axis_size("ent") * ent_dev, ent_dev)
        block_span = max(lax.axis_size("ent") * ent_dev // ent_dev, 1)
        offset = start_row

        def block_term(turn_index):
            row_slots = lax.dynamic_index_in_dim(row_lists, turn_index, 0, keepdims=False)
            col_slots = lax.dynamic_index_in_dim(col_lists, turn_index, 0, keepdims=False)
            live_slots = lax.dynamic_index_in_dim(usable, turn_index, 0, keepdims=False)
            row_hot = hot_table(row_slots, live_slots, 0, sec_dev)
            col_hot = hot_table(col_slots, live_slots, offset, span_width)
            picked = jnp.dot(row_hot, messages, preferred_element_type=jnp.float32).astype(
                jnp.bfloat16
            )
            return jnp.einsum("pw,pf->wf", col_hot, picked, preferred_element_type=jnp.float32)

        pieces = lax.map(block_term, jnp.arange(block_span, dtype=jnp.int32))
        return pieces.reshape(block_span * span_width, feature_width)

    def collect(messages):
        partial_sum = lax.psum_scatter(
            entity_terms(messages, jnp.int32(0)), "ent", scatter_dimension=0, tiled=True
        )
        return lax.psum(partial_sum, "sec")

    zero_sections = jnp.zeros((sec_dev, feature_width), jnp.float32)
    projected = jnp.dot(features, theta, preferred_element_type=jnp.float32)
    scaled = (entity_scale * projected).astype(jnp.bfloat16)
    gathered = entity_fold(
        zero_sections, lax.all_gather(scaled, "ent", axis=0, tiled=True), jnp.int32(0)
    )
    messages = (section_scale * gathered).astype(jnp.bfloat16)
    collected = collect(messages)
    preact = entity_scale * collected
    activated = jax.nn.silu(preact).astype(jnp.bfloat16)
    sigmoid_pre = jax.nn.sigmoid(preact)
    grad_pre = cotangent.astype(jnp.float32) * sigmoid_pre * (1.0 + preact * (1.0 - sigmoid_pre))
    back_scaled = (entity_scale * grad_pre).astype(jnp.bfloat16)
    back_gathered = entity_fold(
        zero_sections, lax.all_gather(back_scaled, "ent", axis=0, tiled=True), jnp.int32(0)
    )
    grad_weight = jnp.sum(gathered * back_gathered, axis=1) / (1.0 + sec_count)
    back_messages = (section_scale * back_gathered).astype(jnp.bfloat16)
    back_collected = collect(back_messages)
    grad_proj = (entity_scale * back_collected).astype(jnp.bfloat16)
    grad_features = lax.dot_general(
        grad_proj, theta, (((1,), (1,)), ((), ())), preferred_element_type=jnp.float32
    ).astype(jnp.bfloat16)
    local_theta = lax.dot_general(
        features, grad_proj, (((0,), (0,)), ((), ())), preferred_element_type=jnp.float32
    )
    grad_theta = lax.psum(local_theta, "ent")
    return (activated, grad_features, grad_theta, grad_weight)


def solution(mesh):
    placed = (
        P("ent", None),
        P(),
        P(("ent", "sec")),
        P(("ent", "sec"), None, None),
        P(("ent", "sec"), None, None),
        P(("ent", "sec"), None),
        P("ent", None),
    )
    return jax.shard_map(
        body,
        mesh=mesh,
        in_specs=placed,
        out_specs=(P("ent", None), P("ent", None), P(), P(("ent", "sec"))),
        check_vma=False,
    )
```

profile of v0, /device:TPU:0, one launch (start us, length us, event | category | flops | bytes accessed | tf_op | source)
XLA Modules:
  0.0 1644.0 jit_solution(5554662827985014451)
XLA Ops:
  9.2 113.5 %scatter_custom_fusion = f32[4096]{0:T(1024)S(1)} fusion(s32[16384]{0:T(1024)S(1)} %bitcast.81, f32[16384]{0:T(1024)S(1)} %bitcast.82, f32[]{:T(128)} %constant.131.clone.1), kind=kCustom, calls=%fused_computation.76 | custom fusion | flops 16384 | bytes 16388 | tf_op jit(solution)/shard_map/scatter-add | solution.py:24
  122.6 68.3 %psum.28 = f32[4096]{0:T(1024)S(1)} all-reduce(f32[4096]{0:T(1024)S(1)} %scatter_custom_fusion), channel_id=1, replica_groups=mesh['ent'=32,'sec'=4] {'ent','sec'}, use_global_device_ids=true, to_apply=%region_1.0 | all-reduce | flops 4096 | bytes 32768 | tf_op jit(solution)/shard_map/psum | solution.py:27
  193.5 113.4 %scatter_custom_fusion.1 = f32[512]{0:T(512)S(1)} fusion(s32[16384]{0:T(1024)S(1)} %bitcast.84, f32[16384]{0:T(1024)S(1)} %bitcast.83, f32[]{:T(128)} %constant.137.clone.1), kind=kCustom, calls=%fused_computation.78 | custom fusion | flops 16384 | bytes 2052 | tf_op jit(solution)/shard_map/scatter-add | solution.py:30
  307.7 79.9 %while.50 = (s32[]{:T(128)}, f32[512,256]{1,0:T(8,128)S(1)}, s32[32,512]{1,0:T(8,128)}, pred[32,512]{1,0:T(8,128)(4,1)S(1)}, s32[32,512]{1,0:T(8,128)}, /*index=...) while((s32[]{:T(128)}, f32[512,256]{1,0:T(8,128)S(1)}, ...), condition=%wide.region_4.5_spmd.clone, body=%wide.region_3.4_spmd.clone.sunk | while | flops 168820736 | bytes 1128617 | solution.py:55
  313.4 1.7 convolution_add_fusion.4
  315.9 1.7 convolution_add_fusion.4
  330.9 1.7 convolution_add_fusion.4
  333.4 1.7 convolution_add_fusion.4
  348.4 1.7 convolution_add_fusion.4
  383.4 1.7 convolution_add_fusion.4
  387.7 2.4 broadcast.21.clone
  390.2 144.5 %while.48 = (s32[]{:T(128)}, f32[32,128,256]{2,1,0:T(8,128)}, s32[32]{0:T(128)S(1)}, s32[32,512]{1,0:T(8,128)}, pred[32,512]{1,0:T(8,128)(4,1)S(1)}, /*index=5*/...) while((s32[]{:T(128)}, f32[32,128,256]{2,1,0:T(8,128)}, ...), condition=%wide.region_6.7_spmd, body=%wide.region_5.6_spmd.sunk | while | flops 168558592 | bytes 408219 | solution.py:73
  534.8 188.6 %reduce-scatter.3.cloned.1.call-done = f32[128,256]{1,0:T(8,128)} async-done(((f32[4096,256]{1,0:T(8,128)}), f32[128,256]{1,0:T(8,128)}) %reduce-scatter.3.cloned.1.call-update) | async-done | bytes 131088 | tf_op jit(solution)/shard_map/reduce_scatter | solution.py:77
  723.4 32.8 %all-reduce.4.cloned.1.call-done = f32[128,256]{1,0:T(8,128)} async-done(((f32[128,256]{1,0:T(8,128)}), f32[128,256]{1,0:T(8,128)}) %all-reduce.4.cloned.1.call-update) | async-done | bytes 131088 | tf_op jit(solution)/shard_map/psum | solution.py:80
  758.0 73.9 %all-gather.5.cloned.1.call-done = bf16[4096,256]{1,0:T(8,128)(2,1)} async-done(((bf16[128,256]{1,0:T(8,128)(2,1)}), bf16[4096,256]{1,0:T(8,128)(2,1)}) %all-gather.5.cloned.1.call-update) | async-done | bytes 2097168 | tf_op jit(solution)/shard_map/all_gather | solution.py:96
  831.9 79.9 %while.51 = (s32[]{:T(128)}, f32[512,256]{1,0:T(8,128)S(1)}, s32[32,512]{1,0:T(8,128)}, pred[32,512]{1,0:T(8,128)(4,1)S(1)}, s32[32,512]{1,0:T(8,128)}, /*index=...) while((s32[]{:T(128)}, f32[512,256]{1,0:T(8,128)S(1)}, ...), condition=%wide.region_10.11_spmd.clone, body=%wide.region_9.10_spmd.clone.sunk | while | flops 168820736 | bytes 1128617 | solution.py:55
  912.0 2.4 broadcast.21
  914.4 144.5 %while.49 = (s32[]{:T(128)}, f32[32,128,256]{2,1,0:T(8,128)}, s32[32]{0:T(128)S(1)}, s32[32,512]{1,0:T(8,128)}, pred[32,512]{1,0:T(8,128)(4,1)S(1)}, /*index=5*/...) while((s32[]{:T(128)}, f32[32,128,256]{2,1,0:T(8,128)}, ...), condition=%wide.region_12.13_spmd, body=%wide.region_11.12_spmd.sunk | while | flops 168558592 | bytes 408219 | solution.py:73
  1059.0 190.6 %reduce-scatter.5.cloned.1.call-done = f32[128,256]{1,0:T(8,128)} async-done(((f32[4096,256]{1,0:T(8,128)}), f32[128,256]{1,0:T(8,128)}) %reduce-scatter.5.cloned.1.call-update) | async-done | bytes 131088 | tf_op jit(solution)/shard_map/reduce_scatter | solution.py:77
  1249.7 32.8 %all-reduce.6.cloned.1.call-done = f32[128,256]{1,0:T(8,128)} async-done(((f32[128,256]{1,0:T(8,128)}), f32[128,256]{1,0:T(8,128)}) %all-reduce.6.cloned.1.call-update) | async-done | bytes 131088 | tf_op jit(solution)/shard_map/psum | solution.py:80
  1282.5 1.9 convolution_bitcast_fusion
  1285.0 1.7 convolution_convert_fusion.4
  1286.8 348.6 %all-reduce.8.cloned.1.call-done = f32[256,256]{0,1:T(8,128)} async-done(((f32[256,256]{0,1:T(8,128)}), f32[256,256]{0,1:T(8,128)}) %all-reduce.8.cloned.1.call-update) | async-done | bytes 262160 | tf_op jit(solution)/shard_map/psum | solution.py:108
  1635.4 1.8 copy.11
  (482 shorter events, 320.6 us)
Async XLA Ops:
  7.2 183.8 %copy-start = (bf16[256,256]{1,0:T(8,128)(2,1)S(1)}, bf16[256,256]{1,0:T(8,128)(2,1)}, u32[]{:S(2)}) copy-start(bf16[256,256]{1,0:T(8,128)(2,1)} %param.16) | copy-start | bytes 393220
  7.2 300.5 %all-gather.3.cloned.1.call-start = ((), (), s32[]{:S(2)}) async-start(), calls=%async_computation.2 | async-start | bytes 2162688 | tf_op jit(solution)/shard_map/all_gather | solution.py:86
  192.6 530.7 %reduce-scatter.3.cloned.1.call-start = ((), (), s32[]{:S(2)}) async-start(), calls=%async_computation.3 | async-start | bytes 4325376 | tf_op jit(solution)/shard_map/reduce_scatter | solution.py:77
  390.1 366.0 %copy-start.2 = (bf16[128,256]{1,0:T(8,128)(2,1)S(1)}, bf16[128,256]{1,0:T(8,128)(2,1)}, u32[]{:S(2)}) copy-start(bf16[128,256]{1,0:T(8,128)(2,1)} %param.21) | copy-start | bytes 196612
  534.7 221.5 %all-reduce.4.cloned.1.call-start = ((), (), s32[]{:S(2)}) async-start(), calls=%async_computation.4 | async-start | bytes 262144 | tf_op jit(solution)/shard_map/psum | solution.py:80
  723.4 108.5 %all-gather.5.cloned.1.call-start = ((), (), s32[]{:S(2)}) async-start(), calls=%async_computation.5 | async-start | bytes 2162688 | tf_op jit(solution)/shard_map/all_gather | solution.py:96
  757.9 491.7 %reduce-scatter.5.cloned.1.call-start = ((), (), s32[]{:S(2)}) async-start(), calls=%async_computation.6 | async-start | bytes 4325376 | tf_op jit(solution)/shard_map/reduce_scatter | solution.py:77
  914.4 368.1 %copy-start.1 = (bf16[128,256]{1,0:T(8,128)(2,1)S(1)}, bf16[128,256]{1,0:T(8,128)(2,1)}, u32[]{:S(2)}) copy-start(bf16[128,256]{1,0:T(8,128)(2,1)} %param.15) | copy-start | bytes 196612
  1059.0 223.6 %all-reduce.6.cloned.1.call-start = ((), (), s32[]{:S(2)}) async-start(), calls=%async_computation.7 | async-start | bytes 262144 | tf_op jit(solution)/shard_map/psum | solution.py:80
  1249.7 385.8 %all-reduce.8.cloned.1.call-start = ((), (), s32[]{:S(2)}) async-start(), calls=%async_computation.8 | async-start | bytes 524288 | tf_op jit(solution)/shard_map/psum | solution.py:108
Sparse Core Ops, SparseCore 0:
  192.7 66.8 all-gather.2
  534.8 188.4 reduce-scatter.2
  725.8 30.3 all-reduce.3
  760.1 71.6 all-gather.4
  1059.1 190.4 reduce-scatter.4
  1252.1 30.3 all-reduce.5
  1285.6 349.7 all-reduce.7
where the time goes:
time: 1670 us; the launch traced here: 1640 us
  waiting for transfers between devices  867 us (52%)
  other arithmetic  231 us (14%)
  matrix products  191 us (11%)
  local copies, waits for them, and re-layouts  145 us (9%)
  loops' own time  126 us (8%)
  blocking collectives  68.3 us (4%)
    reduce_scatter x2, waiting for transfers between devices, collect(): lax.psum_scatter(entity_terms(messages, jnp.int32(0)), 'ent', scatter_dim...  379 us
    psum x1, waiting for transfers between devices, body(): grad_theta = lax.psum(local_theta, 'ent')  349 us
    another operation x2, loops' own time, entity_terms(): pieces = lax.map(block_term, jnp.arange(block_span, dtype=jnp.int32))  125 us
    scatter-add x1, other arithmetic, body(): jax.ops.segment_sum(usable_float.reshape(-1), entity_index.reshape(-1), n...  113 us
    scatter-add x1, other arithmetic, body(): jax.ops.segment_sum(usable_float.reshape(-1), row_lists.reshape(-1), num_...  113 us
    dot_general x64, matrix products, add_block(): jnp.einsum('ps,pf->sf', row_hot, picked, preferred_element_type=jnp.float32)  108 us
    dot_general x64, matrix products, block_term(): jnp.einsum('pw,pf->wf', col_hot, picked, preferred_element_type=jnp.float32)  77.7 us
    all_gather x1, waiting for transfers between devices, body(): lax.all_gather(back_scaled, 'ent', axis=0, tiled=True)  73.9 us
  transfers between devices with their start and end apart: 7, of which 6 were waited for; matrix products, arithmetic and copies ran while one was open for 7% of the time, Pallas kernels for 0%

commit v1 on v0

--- a/solution.py
+++ b/solution.py
@@ -93,7 +93,11 @@
     grad_pre = cotangent.astype(jnp.float32) * sigmoid_pre * (1.0 + preact * (1.0 - sigmoid_pre))
     back_scaled = (entity_scale * grad_pre).astype(jnp.bfloat16)
     back_gathered = entity_fold(
-        zero_sections, lax.all_gather(back_scaled, "ent", axis=0, tiled=True), jnp.int32(0)
+        zero_sections,
+        jnp.concatenate(
+            lax.all_to_all(jnp.stack([back_scaled] * lax.axis_size("ent")), "ent", 0, 0), axis=0
+        ),
+        jnp.int32(0),
     )
     grad_weight = jnp.sum(gathered * back_gathered, axis=1) / (1.0 + sec_count)
     back_messages = (section_scale * back_gathered).astype(jnp.bfloat16)

time: 1670 us -> 1610 us (0.964)
  waiting for transfers between devices: 867 us -> 823 us
  matrix products: 191 us -> 165 us
    all_gather x1 -> x0, waiting for transfers between devices: 73.9 us -> none  [body(): lax.all_gather(back_scaled, 'ent', axis=0, tiled=True)]
    all_to_all x0 -> x1, waiting for transfers between devices: none -> 29 us  [body(): lax.all_to_all(jnp.stack([back_scaled] * lax.axis_size('ent')), 'ent', 0, 0)]
    dot_general x64, matrix products: 108 us -> 81.6 us  [add_block(): jnp.einsum('ps,pf->sf', row_hot, picked, preferred_element_type=jnp.float32)]
where the time goes in v1:
time: 1610 us; the launch traced here: 1580 us
  waiting for transfers between devices  823 us (51%)
  other arithmetic  231 us (14%)
  matrix products  165 us (10%)
  local copies, waits for them, and re-layouts  147 us (9%)
  loops' own time  126 us (8%)
  blocking collectives  68.3 us (4%)
    reduce_scatter x2, waiting for transfers between devices, collect(): lax.psum_scatter(entity_terms(messages, jnp.int32(0)), 'ent', scatter_dim...  379 us
    psum x1, waiting for transfers between devices, body(): grad_theta = lax.psum(local_theta, 'ent')  349 us
    another operation x2, loops' own time, entity_terms(): pieces = lax.map(block_term, jnp.arange(block_span, dtype=jnp.int32))  125 us
    scatter-add x1, other arithmetic, body(): jax.ops.segment_sum(usable_float.reshape(-1), entity_index.reshape(-1), n...  113 us
    scatter-add x1, other arithmetic, body(): jax.ops.segment_sum(usable_float.reshape(-1), row_lists.reshape(-1), num_...  113 us
    dot_general x64, matrix products, add_block(): jnp.einsum('ps,pf->sf', row_hot, picked, preferred_element_type=jnp.float32)  81.6 us
    dot_general x64, matrix products, block_term(): jnp.einsum('pw,pf->wf', col_hot, picked, preferred_element_type=jnp.float32)  77.7 us
    psum x1, blocking collectives, body(): entity_degree = lax.psum(local_degree, ('ent', 'sec'))  68.3 us
  transfers between devices with their start and end apart: 7, of which 6 were waited for; matrix products, arithmetic and copies ran while one was open for 7% of the time, Pallas kernels for 0%

profile of v1, /device:TPU:0, one launch (start us, length us, event | category | flops | bytes accessed | tf_op | source)
XLA Modules:
  0.0 1583.2 jit_solution(12497327170666534477)
XLA Ops:
  9.2 113.5 %scatter_custom_fusion = f32[4096]{0:T(1024)S(1)} fusion(s32[16384]{0:T(1024)S(1)} %bitcast.83, f32[16384]{0:T(1024)S(1)} %bitcast.84, f32[]{:T(128)} %constant.131.clone.1), kind=kCustom, calls=%fused_computation.76 | custom fusion | flops 16384 | bytes 16388 | tf_op jit(solution)/shard_map/scatter-add | solution.py:24
  122.6 68.3 %psum.28 = f32[4096]{0:T(1024)S(1)} all-reduce(f32[4096]{0:T(1024)S(1)} %scatter_custom_fusion), channel_id=1, replica_groups=mesh['ent'=32,'sec'=4] {'ent','sec'}, use_global_device_ids=true, to_apply=%region_1.0 | all-reduce | flops 4096 | bytes 32768 | tf_op jit(solution)/shard_map/psum | solution.py:27
  193.5 113.4 %scatter_custom_fusion.1 = f32[512]{0:T(512)S(1)} fusion(s32[16384]{0:T(1024)S(1)} %bitcast.86, f32[16384]{0:T(1024)S(1)} %bitcast.85, f32[]{:T(128)} %constant.137.clone.1), kind=kCustom, calls=%fused_computation.78 | custom fusion | flops 16384 | bytes 2052 | tf_op jit(solution)/shard_map/scatter-add | solution.py:30
  307.7 79.9 %while.50 = (s32[]{:T(128)}, f32[512,256]{1,0:T(8,128)S(1)}, s32[32,512]{1,0:T(8,128)}, pred[32,512]{1,0:T(8,128)(4,1)S(1)}, s32[32,512]{1,0:T(8,128)}, /*index=...) while((s32[]{:T(128)}, f32[512,256]{1,0:T(8,128)S(1)}, ...), condition=%wide.region_4.5_spmd.clone, body=%wide.region_3.4_spmd.clone.sunk | while | flops 168820736 | bytes 1128617 | solution.py:55
  313.4 1.7 convolution_add_fusion.4
  315.9 1.7 convolution_add_fusion.4
  318.4 1.7 convolution_add_fusion.4
  320.9 1.7 convolution_add_fusion.4
  323.4 1.7 convolution_add_fusion.4
  387.7 2.4 broadcast.23.clone
  390.1 144.5 %while.48 = (s32[]{:T(128)}, f32[32,128,256]{2,1,0:T(8,128)}, s32[32]{0:T(128)S(1)}, s32[32,512]{1,0:T(8,128)}, pred[32,512]{1,0:T(8,128)(4,1)S(1)}, /*index=5*/...) while((s32[]{:T(128)}, f32[32,128,256]{2,1,0:T(8,128)}, ...), condition=%wide.region_6.7_spmd, body=%wide.region_5.6_spmd.sunk | while | flops 168558592 | bytes 408219 | solution.py:73
  534.7 188.6 %reduce-scatter.3.cloned.1.call-done = f32[128,256]{1,0:T(8,128)} async-done(((f32[4096,256]{1,0:T(8,128)}), f32[128,256]{1,0:T(8,128)}) %reduce-scatter.3.cloned.1.call-update) | async-done | bytes 131088 | tf_op jit(solution)/shard_map/reduce_scatter | solution.py:77
  723.3 32.8 %all-reduce.4.cloned.1.call-done = f32[128,256]{1,0:T(8,128)} async-done(((f32[128,256]{1,0:T(8,128)}), f32[128,256]{1,0:T(8,128)}) %all-reduce.4.cloned.1.call-update) | async-done | bytes 131088 | tf_op jit(solution)/shard_map/psum | solution.py:80
  759.4 9.4 all-to-all-start
  768.9 29.0 %all-to-all-done = bf16[32,128,256]{2,1,0:T(8,128)(2,1)S(1)} async-done(((bf16[32,128,256]{2,1,0:T(8,128)(2,1)}), bf16[32,128,256]{2,1,0:T(8,128)(2,1)S(1)}, u32[]{:S(2)}, u32[]{:S(2)}) %all-to-all-start) | async-done | bytes 2097184 | tf_op jit(solution)/shard_map/all_to_all | solution.py:98
  797.8 53.0 %while.51 = (s32[]{:T(128)}, f32[512,256]{1,0:T(8,128)S(1)}, s32[32,512]{1,0:T(8,128)}, pred[32,512]{1,0:T(8,128)(4,1)S(1)}, s32[32,512]{1,0:T(8,128)}, /*index=...) while((s32[]{:T(128)}, f32[512,256]{1,0:T(8,128)S(1)}, ...), condition=%wide.region_10.11_spmd.clone, body=%wide.region_9.10_spmd.clone.sunk | while | flops 168820736 | bytes 1128617 | solution.py:55
  851.1 2.4 broadcast.23
  853.5 144.5 %while.49 = (s32[]{:T(128)}, f32[32,128,256]{2,1,0:T(8,128)}, s32[32]{0:T(128)S(1)}, s32[32,512]{1,0:T(8,128)}, pred[32,512]{1,0:T(8,128)(4,1)S(1)}, /*index=5*/...) while((s32[]{:T(128)}, f32[32,128,256]{2,1,0:T(8,128)}, ...), condition=%wide.region_12.13_spmd, body=%wide.region_11.12_spmd.sunk | while | flops 168558592 | bytes 408219 | solution.py:73
  998.1 190.9 %reduce-scatter.5.cloned.1.call-done = f32[128,256]{1,0:T(8,128)} async-done(((f32[4096,256]{1,0:T(8,128)}), f32[128,256]{1,0:T(8,128)}) %reduce-scatter.5.cloned.1.call-update) | async-done | bytes 131088 | tf_op jit(solution)/shard_map/reduce_scatter | solution.py:77
  1189.0 32.7 %all-reduce.6.cloned.1.call-done = f32[128,256]{1,0:T(8,128)} async-done(((f32[128,256]{1,0:T(8,128)}), f32[128,256]{1,0:T(8,128)}) %all-reduce.6.cloned.1.call-update) | async-done | bytes 131088 | tf_op jit(solution)/shard_map/psum | solution.py:80
  1221.8 1.9 convolution_bitcast_fusion
  1224.3 1.7 convolution_convert_fusion.4
  1226.0 348.5 %all-reduce.8.cloned.1.call-done = f32[256,256]{0,1:T(8,128)} async-done(((f32[256,256]{0,1:T(8,128)}), f32[256,256]{0,1:T(8,128)}) %all-reduce.8.cloned.1.call-update) | async-done | bytes 262160 | tf_op jit(solution)/shard_map/psum | solution.py:112
  1574.5 1.8 copy.11
  (482 shorter events, 296.9 us)
Async XLA Ops:
  7.2 183.8 %copy-start = (bf16[256,256]{1,0:T(8,128)(2,1)S(1)}, bf16[256,256]{1,0:T(8,128)(2,1)}, u32[]{:S(2)}) copy-start(bf16[256,256]{1,0:T(8,128)(2,1)} %param.16) | copy-start | bytes 393220
  7.2 300.5 %all-gather.2.cloned.1.call-start = ((), (), s32[]{:S(2)}) async-start(), calls=%async_computation.3 | async-start | bytes 2162688 | tf_op jit(solution)/shard_map/all_gather | solution.py:86
  192.6 530.7 %reduce-scatter.3.cloned.1.call-start = ((), (), s32[]{:S(2)}) async-start(), calls=%async_computation.4 | async-start | bytes 4325376 | tf_op jit(solution)/shard_map/reduce_scatter | solution.py:77
  390.1 366.0 %copy-start.2 = (bf16[128,256]{1,0:T(8,128)(2,1)S(1)}, bf16[128,256]{1,0:T(8,128)(2,1)}, u32[]{:S(2)}) copy-start(bf16[128,256]{1,0:T(8,128)(2,1)} %param.21) | copy-start | bytes 196612
  534.7 221.5 %all-reduce.4.cloned.1.call-start = ((), (), s32[]{:S(2)}) async-start(), calls=%async_computation.5 | async-start | bytes 262144 | tf_op jit(solution)/shard_map/psum | solution.py:80
  759.4 38.4 %all-to-all-start = ((bf16[32,128,256]{2,1,0:T(8,128)(2,1)}), bf16[32,128,256]{2,1,0:T(8,128)(2,1)S(1)}, u32[]{:S(2)}, u32[]{:S(2)}) async-start(bf16[32,128,256]{2,1,0:T(8,128)(2,1)} %stack.2), calls=%async_computation.1 | async-start | bytes 4194304 | tf_op jit(solution)/shard_map/all_to_all | solution.py:98
  768.8 420.2 %reduce-scatter.5.cloned.1.call-start = ((), (), s32[]{:S(2)}) async-start(), calls=%async_computation.6 | async-start | bytes 4325376 | tf_op jit(solution)/shard_map/reduce_scatter | solution.py:77
  853.5 368.2 %copy-start.1 = (bf16[128,256]{1,0:T(8,128)(2,1)S(1)}, bf16[128,256]{1,0:T(8,128)(2,1)}, u32[]{:S(2)}) copy-start(bf16[128,256]{1,0:T(8,128)(2,1)} %param.15) | copy-start | bytes 196612
  998.1 223.7 %all-reduce.6.cloned.1.call-start = ((), (), s32[]{:S(2)}) async-start(), calls=%async_computation.7 | async-start | bytes 262144 | tf_op jit(solution)/shard_map/psum | solution.py:80
  1189.0 385.5 %all-reduce.8.cloned.1.call-start = ((), (), s32[]{:S(2)}) async-start(), calls=%async_computation.8 | async-start | bytes 524288 | tf_op jit(solution)/shard_map/psum | solution.py:112
Sparse Core Ops, SparseCore 0:
  192.7 66.8 all-gather.1
  534.8 188.4 reduce-scatter.2
  725.8 30.3 all-reduce.3
  998.2 190.7 reduce-scatter.4
  1191.4 30.2 all-reduce.5
  1224.7 349.8 all-reduce.7
